TPU v7x, 128 devices: a whole 4x4x4 slice. The times are simulated.
128 devices in a mesh: angle: 16 (over y, x), block: 8 (over z, core).
Axes of the slice: x: 4, y: 4, z: 4, core: 2. Of those that a mesh axis runs over, the one named last changes fastest.
Arguments:
- object_field: float32 [32, 2, 512, 512], P(None, None, 'block'), may hold values from -1.5 to 1.5
- shears: int32 [16, 32], P('angle'), may hold values from -16 to 16, as said below
- positions: int32 [16, 8, 2], P('angle', 'block'), may hold values from 0 to 511
- measured: bfloat16 [16, 8, 512, 512], P('angle', 'block'), may hold values from 0 to 2
- probe_field: float32 [2, 512, 512], replicated
- kappa_field: float32 [16, 512, 512], P('angle'), may hold values from 0.01 to 0.1
Outputs:
- updated_object: float32 [32, 2, 512, 512], P(None, None, 'block')
Inputs may be any that keep to these rules, and one draw needn't show every extreme that they name: `shears`: each angle's row offset of each slice; the values -16 and 16 occur in every draw.
All inputs are finite; a program needn't handle non-finite values.
Results may differ from a plain program's by a relative error of at most 0.0003.
Values sent between devices are 32-bit elements; how exact they have to be, the bound alone decides.
No kernel may reach another device: no remote copies, remote signals or barrier semaphores. Data moves between devices by JAX's collectives and lax.ppermute only.
A program may use at most 192 MiB of HBM per device.

v0:
```python
import jax
import jax.numpy as jnp
from jax import lax
from jax.sharding import PartitionSpec as P

NX = 512
NY = 512
STEPS = 2
SH = 16


def with_halo(x, sides, width):
    for axis, dim in sides:
        count, length = (lax.axis_size(axis), x.shape[dim])
        up = [(i, (i + 1) % count) for i in range(count)]
        down = [(j, i) for i, j in up]
        last = lax.slice_in_dim(x, length - width, length, axis=dim)
        first = lax.slice_in_dim(x, 0, width, axis=dim)
        before = lax.ppermute(last, axis, up)
        after = lax.ppermute(first, axis, down)
        x = jnp.concatenate([before, x, after], axis=dim)
    return x


def laplace(field):
    return (
        jnp.roll(field, 1, -2)
        + jnp.roll(field, -1, -2)
        + jnp.roll(field, 1, -1)
        + jnp.roll(field, -1, -1)
        - 4.0 * field
    )


def frame_loss(projected, probe_field, kappa_row, offset, observed):
    window = jnp.roll(projected, (-offset[0], -offset[1]), axis=(1, 2))
    real_part = probe_field[0] * window[0] - probe_field[1] * window[1]
    imag_part = probe_field[0] * window[1] + probe_field[1] * window[0]
    for step in range(STEPS):
        real_part, imag_part = (
            real_part - kappa_row * laplace(imag_part),
            imag_part + kappa_row * laplace(real_part),
        )
    misfit = real_part * real_part + imag_part * imag_part - observed.astype(jnp.float32)
    return 0.5 * jnp.sum(misfit * misfit)


def per_device(object_field, shears, positions, measured, probe_field, kappa_field):
    strip_rows = object_field.shape[2]
    shear_row = shears[0]
    extended = with_halo(object_field, (("block", 2),), SH)

    def slice_rows(slab, amount):
        return lax.dynamic_slice_in_dim(slab, SH + amount, strip_rows, 1)

    own_strip = jnp.sum(jax.vmap(slice_rows)(extended, shear_row), axis=0)
    projected = lax.all_gather(own_strip, "block", axis=1, tiled=True)
    intensity = probe_field[0] * probe_field[0] + probe_field[1] * probe_field[1]
    kappa_row = kappa_field[0]

    def per_frame(totals, frame_in):
        offset, observed = frame_in
        grads = jax.grad(frame_loss)(projected, probe_field, kappa_row, offset, observed)
        weight = jnp.roll(intensity, (offset[0], offset[1]), axis=(0, 1))
        return (totals + jnp.concatenate([grads, weight[None]], 0), None)

    totals, _ = lax.scan(
        per_frame, jnp.zeros((3, NX, NY), jnp.float32), (positions[0], measured[0])
    )
    strip_totals = lax.psum_scatter(totals, "block", scatter_dimension=1, tiled=True)
    gradient_rim = with_halo(strip_totals, (("block", 1),), SH)

    def unshear_rows(rim_block, amount):
        return lax.dynamic_slice_in_dim(rim_block, SH - amount, strip_rows, 1)

    unsheared = jax.vmap(lambda amount: unshear_rows(gradient_rim, amount))(shear_row)
    summed = lax.psum(unsheared, "angle")
    return object_field - summed[:, :2] / (summed[:, 2:3] + 1.0)


def solution(mesh):
    placed = (
        P(None, None, "block", None),
        P("angle", None),
        P("angle", "block", None),
        P("angle", "block", None, None),
        P(),
        P("angle", None, None),
    )
    return jax.shard_map(
        per_device,
        mesh=mesh,
        in_specs=placed,
        out_specs=P(None, None, "block", None),
        check_vma=False,
    )
```

profile of v0, /device:TPU:1, one launch (start us, length us, event | category | flops | bytes accessed | tf_op | source)
XLA Modules:
  0.0 588.4 jit_solution(2454463777330651448)
XLA Ops:
  6.5 14.3 %copy.27 = f32[32,2,64,512]{3,1,0,2:T(2,128)S(1)} copy(f32[32,2,64,512]{3,2,1,0:T(8,128)} %param.6) | data formatting | bytes 16777216 | tf_op args[0]
  20.9 2.3 fusion.41
  23.2 3.0 collective-permute-start
  26.2 23.0 %collective-permute-done = f32[32,2,16,512]{3,1,0,2:T(2,128)S(1)} collective-permute-done((f32[32,2,16,512]{3,1,0,2:T(2,128)S(1)}, f32[32,2,16,512]{3,1,0,2:T(2,128)S(1)}, u32[]{:S(2)}, u32[]{:S(2)}) %collective-permute-start) | collective-permute-done | bytes 2097184 | tf_op jit(solution)/shard_map/ppermute | solution.py:19
  49.2 2.5 collective-permute-done.1
  51.7 26.0 %pad_maximum_fusion = f32[32,2,96,512]{3,1,0,2:T(2,128)} fusion(f32[32,2,16,512]{3,1,0,2:T(2,128)S(1)} %collective-permute-done.1, f32[32,2,64,512]{3,1,0,2:T(2,128)S(1)} %copy.27, f32[32,2,16,512]{3,1,0,2:T(2,128)S(1)} %collective-permute-done), kind=kLoop, calls=%fused_computation.2 | loop fusion | flops 6291456 | bytes 25165824 | tf_op jit(solution)/shard_map/concatenate | solution.py:21
  77.7 16.2 %gather_fusion.1 = f32[32,2,64,512]{3,1,2,0:T(2,128)} fusion(f32[32,2,96,512]{3,1,0,2:T(2,128)} %pad_maximum_fusion, s32[32]{0:T(128)S(1)} %get-tuple-element.115), kind=kCustom, calls=%fused_computation.1 | custom fusion | bytes 16777728 | tf_op jit(solution)/shard_map/vmap()/gather | solution.py:54
  94.0 6.8 %reduce_sum.9 = f32[2,64,512]{2,0,1:T(2,128)} reduce(f32[32,2,64,512]{3,1,2,0:T(2,128)} %gather_fusion.1, f32[]{:T(128)} %constant.99.clone.1), dimensions={0}, to_apply=%region_0.0 | reduce | flops 2031616 | bytes 8650756 | tf_op jit(solution)/shard_map/reduce_sum | solution.py:56
  100.8 0.3 all-reduce.42.cloned.1.call-start
  101.1 0.6 fusion.75
  106.7 21.5 %all-gather.2.cloned.1.call-done = f32[2,512,512]{2,0,1:T(2,128)} async-done(((f32[2,64,512]{2,0,1:T(2,128)}), f32[2,512,512]{2,0,1:T(2,128)}) %all-gather.2.cloned.1.call-update) | async-done | bytes 2097168 | tf_op jit(solution)/shard_map/all_gather | solution.py:57
  128.2 5.8 fusion.3
  133.9 4.5 fusion.2
  138.4 1.6 fusion.42
  140.0 0.5 fusion.27
  140.5 0.4 fusion.71
  140.9 0.2 fusion.73
  141.3 0.4 copy-done
  141.8 12.8 %fusion.16 = (f32[512,512]{1,0:T(8,128)S(1)}, f32[512,512]{1,0:T(8,128)S(1)}) fusion(f32[511,512]{1,0:T(8,128)S(1)} %get-tuple-element.111, f32[1,512]{1,0:T(1,128)S(1)} %get-tuple-element.113, f32[1,512]{1,0:T(1,128)S(1)} %get-tuple-element.112, f32[511,512]{1,0:T(8,128)S(1)} %get-tuple-element.110, f32[512,511]{1,0:T(8,128)S(1)} %get-tuple-element.107, ...), kind=kLoop, calls=%fused_computation.35 | loop fusion | flops 3670016 | bytes 12582912 | tf_op jit(solution)/shard_map/while/body/eval_jaxpr/jvp()/sub | solution.py:41
  154.8 0.7 fusion.62
  155.5 0.3 fusion.60
  155.9 1.0 fusion.11
  156.9 0.2 fusion.64
  157.1 0.4 fusion.66
  157.7 0.2 copy-done.3
  157.9 2.3 bitcast_multiply_fusion.5
  160.3 0.4 bitcast_multiply_fusion.4
  160.7 0.4 fusion.56
  161.0 0.2 fusion.58
  161.4 1.2 bitcast_multiply_fusion.3
  162.6 0.4 fusion.52
  163.0 0.2 fusion.54
  163.4 0.4 fusion.48
  163.8 0.2 fusion.50
  164.1 2.4 fusion.34
  166.5 0.2 bitcast_multiply_fusion.2
  166.7 0.4 fusion.44
  167.1 0.2 fusion.46
  167.5 1.0 fusion.35
  168.5 0.5 fusion.31
  169.0 0.5 pad_add_fusion
  169.5 1.6 copy.31
  171.1 3.1 broadcast_in_dim.37
  174.2 96.8 %dynamic_update_slice.10 = f32[2,512,1024]{2,0,1:T(2,128)} dynamic-update-slice(f32[2,512,1024]{2,0,1:T(2,128)} %broadcast_in_dim.37, f32[2,512,512]{2,0,1:T(2,128)S(1)} %copy.31, s32[]{:T(128)} %constant.100.clone.1, s32[]{:T(128)} %constant.100.clone.1, s32[]{:T(128)S(6)} %select_n.79) | dynamic-update-slice | bytes 4194308 | tf_op jit(solution)/shard_map/while/body/eval_jaxpr/transpose(jvp(jit(_roll_dynamic)))/dynamic_update_slice | solution.py:36
  271.1 1.1 broadcast_in_dim.36
  272.2 1.1 copy-done.2
  273.3 1.2 fusion.4
  274.5 1.1 slice_add_fusion.1
  275.6 0.5 fusion.6
  276.1 0.6 fusion.5
  276.7 0.7 broadcast_in_dim.42
  277.4 3.9 pad_maximum_fusion.1
  281.4 0.6 dynamic-slice
  282.6 70.1 %all-reduce.42.cloned.1.call-done = f32[3,512,512]{2,0,1:T(4,128)} async-done(((f32[3,512,512]{2,0,1:T(4,128)}), f32[3,512,512]{2,0,1:T(4,128)}) %all-reduce.42.cloned.1.call-update) | async-done | bytes 3145744
  352.6 1.0 constant_dynamic-slice_fusion.1
  353.7 0.9 collective-permute-start.2
  354.5 1.6 collective-permute-start.3
  356.1 1.1 constant_dynamic-slice_fusion.2
  357.3 1.7 collective-permute-done.3
  359.1 12.3 %gather_fusion = f32[32,3,64,512]{3,1,2,0:T(4,128)} fusion(f32[3,96,512]{2,0,1:T(4,128)S(1)} %pad_maximum_fusion.2, s32[32]{0:T(128)S(1)} %get-tuple-element.114), kind=kCustom, calls=%fused_computation | custom fusion | bytes 25166208 | tf_op jit(solution)/shard_map/vmap()/gather | solution.py:74
  371.4 15.5 %copy.32 = f32[32,3,64,512]{3,2,1,0:T(8,128)} copy(f32[32,3,64,512]{3,1,2,0:T(4,128)} %gather_fusion) | data formatting | bytes 25165824 | tf_op jit(solution)/shard_map/vmap()/gather | solution.py:74
  387.0 182.0 %all-reduce.40.cloned.1.call-done = f32[32,3,64,512]{3,2,1,0:T(8,128)} async-done(((f32[32,3,64,512]{3,2,1,0:T(8,128)}), f32[32,3,64,512]{3,2,1,0:T(8,128)}) %all-reduce.40.cloned.1.call-update) | async-done | bytes 12582928 | tf_op jit(solution)/shard_map/psum | solution.py:77
  569.0 2.9 fusion.1
  571.9 9.6 %fusion = f32[32,2,64,512]{3,2,1,0:T(8,128)} fusion(f32[32,2,64,512]{3,2,1,0:T(8,128)} %param.6, f32[32,3,64,512]{3,2,1,0:T(8,128)} %all-reduce.40.cloned.1.call-done, f32[32,64,512]{2,1,0:T(8,128)S(1)} %fusion.1), kind=kLoop, calls=%fused_computation.4 | loop fusion | flops 4194304 | bytes 29360128 | tf_op jit(solution)/shard_map/sub | solution.py:78
  (34 shorter events, 1.4 us)
Async XLA Ops:
  6.5 121.6 %all-gather.2.cloned.1.call-start = ((), (), s32[]{:S(2)}) async-start(), calls=%async_computation | async-start | bytes 2359296 | tf_op jit(solution)/shard_map/all_gather | solution.py:57
  20.9 5.4 copy-start.5
  23.2 26.0 %collective-permute-start = (f32[32,2,16,512]{3,1,0,2:T(2,128)S(1)}, f32[32,2,16,512]{3,1,0,2:T(2,128)S(1)}, u32[]{:S(2)}, u32[]{:S(2)}) collective-permute-start(f32[32,2,16,512]{3,1,0,2:T(2,128)S(1)} %get-tuple-element.41), channel_id=1, source_target_pairs={{0,1},{1,2},{2,3},{3,4},{4,5},{5,6},{6,7},{7,0},{8,9},{9,10},{10,1... | collective-permute-start | bytes 6291464 | tf_op jit(solution)/shard_map/ppermute | solution.py:19
  26.2 25.5 %collective-permute-start.1 = (f32[32,2,16,512]{3,1,0,2:T(2,128)S(1)}, f32[32,2,16,512]{3,1,0,2:T(2,128)S(1)}, u32[]{:S(2)}, u32[]{:S(2)}) collective-permute-start(f32[32,2,16,512]{3,1,0,2:T(2,128)S(1)} %get-tuple-element.42), channel_id=1, source_target_pairs={{1,0},{2,1},{3,2},{4,3},{5,4},{6,5},{7,6},{0,7},{9,8},{10,9},{11,1... | collective-permute-start | bytes 6291464 | tf_op jit(solution)/shard_map/ppermute | solution.py:20
  94.0 7.2 %copy-start.4 = (s32[1,1,2]{2,1,0:T(1,128)S(1)}, s32[1,1,2]{2,1,0:T(1,128)}, u32[]{:S(2)}) copy-start(s32[1,1,2]{2,1,0:T(1,128)} %param.8) | copy-start | bytes 28
  100.8 251.8 %all-reduce.42.cloned.1.call-start = ((), (), s32[]{:S(2)}) async-start(), calls=%async_computation.2 | async-start | bytes 8388608
  133.9 6.1 %copy-start.1 = (f32[2,512,512]{2,1,0:T(8,128)S(1)}, f32[2,512,512]{2,1,0:T(8,128)}, u32[]{:S(2)}) copy-start(f32[2,512,512]{2,1,0:T(8,128)} %param.10) | copy-start | bytes 6291460
  140.5 1.2 copy-start
  156.9 1.0 copy-start.3
  271.1 2.2 copy-start.2
  277.4 4.0 copy-start.6
  281.4 287.6 %all-reduce.40.cloned.1.call-start = ((), (), s32[]{:S(2)}) async-start(), calls=%async_computation.1 | async-start | bytes 25165824 | tf_op jit(solution)/shard_map/psum | solution.py:77
  353.7 3.6 collective-permute-start.2
  354.5 4.4 collective-permute-start.3
Sparse Core Ops, SparseCore 0:
  100.9 27.1 all-gather.1
  281.5 71.1 all-reduce.41
  387.1 181.8 all-reduce.39
where the time goes:
time: 600 us; the launch traced here: 588 us
  waiting for transfers between devices  301 us (50%)
  local copies, waits for them, and re-layouts  177 us (30%)
  other arithmetic  85.7 us (14%)
  between operations  19.5 us (3%)
    psum x1, waiting for transfers between devices, per_device(): summed = lax.psum(unsheared, 'angle')  182 us
    dynamic_update_slice x1, local copies, waits for them, and re-layouts, frame_loss(): window = jnp.roll(projected, (-offset[0], -offset[1]), axis=(1, 2))  96.8 us
    unnamed x4, waiting for transfers between devices  70.1 us
    gather x2, local copies, waits for them, and re-layouts, unshear_rows(): return lax.dynamic_slice_in_dim(rim_block, SH - amount, strip_rows, 1)  27.8 us
    concatenate x2, other arithmetic, with_halo(): x = jnp.concatenate([before, x, after], axis=dim)  26.2 us
    ppermute x2, waiting for transfers between devices, with_halo(): before = lax.ppermute(last, axis, up)  23 us
    all_gather x1, waiting for transfers between devices, per_device(): projected = lax.all_gather(own_strip, 'block', axis=1, tiled=True)  21.5 us
    unnamed x17, local copies, waits for them, and re-layouts  17.8 us
  transfers between devices with their start and end apart: 7, of which 6 were waited for; matrix products, arithmetic and copies ran while one was open for 0% of the time, Pallas kernels for 0%

commit v1 on v0

--- a/solution.py
+++ b/solution.py
@@ -74,7 +74,9 @@
         return lax.dynamic_slice_in_dim(rim_block, SH - amount, strip_rows, 1)
 
     unsheared = jax.vmap(lambda amount: unshear_rows(gradient_rim, amount))(shear_row)
-    summed = lax.psum(unsheared, "angle")
+    summed = unsheared
+    for hop in (1, 2, 4, 8):
+        summed = summed + lax.ppermute(summed, "angle", [(dev, dev ^ hop) for dev in range(16)])
     return object_field - summed[:, :2] / (summed[:, 2:3] + 1.0)
 
 

time: 600 us -> 1520 us (2.53)
  waiting for transfers between devices: 301 us -> 1180 us
    ppermute x0 -> x4, waiting for transfers between devices: none -> 1060 us  [per_device(): lax.ppermute(summed, 'angle', [(dev, dev ^ hop) for dev in range(16)])]
    psum x1 -> x0, waiting for transfers between devices: 182 us -> none  [per_device(): summed = lax.psum(unsheared, 'angle')]
    add x0 -> x4, other arithmetic: none -> 30.1 us  [per_device(): summed + lax.ppermute(summed, 'angle', [(dev, dev ^ hop) for dev in range...]
    unnamed x4 -> x3, waiting for transfers between devices: 70.1 us -> 70.1 us
  transfers between devices with their start and end apart: 7 -> 10, of which waited for: 6 -> 9; matrix products, arithmetic and copies ran while one was open for 0% -> 0% of each run, Pallas kernels for 0% -> 0%
where the time goes in v1:
time: 1520 us; the launch traced here: 1500 us
  waiting for transfers between devices  1180 us (78%)
  local copies, waits for them, and re-layouts  178 us (12%)
  other arithmetic  100 us (7%)
  between operations  19.9 us (1%)
    ppermute x4, waiting for transfers between devices, per_device(): lax.ppermute(summed, 'angle', [(dev, dev ^ hop) for dev in range(16)])  1060 us
    dynamic_update_slice x1, local copies, waits for them, and re-layouts, frame_loss(): window = jnp.roll(projected, (-offset[0], -offset[1]), axis=(1, 2))  96.8 us
    unnamed x3, waiting for transfers between devices  70.1 us
  transfers between devices with their start and end apart: 10, of which 9 were waited for; matrix products, arithmetic and copies ran while one was open for 0% of the time, Pallas kernels for 0%

profile of v1, /device:TPU:1, one launch (start us, length us, event | category | flops | bytes accessed | tf_op | source)
XLA Modules:
  0.0 1495.6 jit_solution(3520145131465070882)
XLA Ops:
  6.5 14.3 copy.43
  20.9 2.3 fusion.41
  23.2 3.0 collective-permute-start
  26.2 23.0 %collective-permute-done = f32[32,2,16,512]{3,1,0,2:T(2,128)S(1)} collective-permute-done((f32[32,2,16,512]{3,1,0,2:T(2,128)S(1)}, f32[32,2,16,512]{3,1,0,2:T(2,128)S(1)}, u32[]{:S(2)}, u32[]{:S(2)}) %collective-permute-start) | collective-permute-done | bytes 2097184 | tf_op jit(solution)/shard_map/ppermute | solution.py:19
  49.2 2.5 collective-permute-done.1
  51.7 25.9 %pad_maximum_fusion = f32[32,2,96,512]{3,1,0,2:T(2,128)} fusion(f32[32,2,16,512]{3,1,0,2:T(2,128)S(1)} %collective-permute-done.1, f32[32,2,64,512]{3,1,0,2:T(2,128)S(1)} %copy.43, f32[32,2,16,512]{3,1,0,2:T(2,128)S(1)} %collective-permute-done), kind=kLoop, calls=%fused_computation.2 | loop fusion | flops 6291456 | bytes 25165824 | tf_op jit(solution)/shard_map/concatenate | solution.py:21
  77.6 16.2 %gather_fusion.1 = f32[32,2,64,512]{3,1,2,0:T(2,128)} fusion(f32[32,2,96,512]{3,1,0,2:T(2,128)} %pad_maximum_fusion, s32[32]{0:T(128)S(1)} %get-tuple-element.115), kind=kCustom, calls=%fused_computation.1 | custom fusion | bytes 16777728 | tf_op jit(solution)/shard_map/vmap()/gather | solution.py:54
  93.9 6.8 reduce_sum.9
  100.9 0.6 fusion.75
  106.4 21.6 %all-gather.2.cloned.1.call-done = f32[2,512,512]{2,0,1:T(2,128)} async-done(((f32[2,64,512]{2,0,1:T(2,128)}), f32[2,512,512]{2,0,1:T(2,128)}) %all-gather.2.cloned.1.call-update) | async-done | bytes 2097168 | tf_op jit(solution)/shard_map/all_gather | solution.py:57
  128.1 5.8 fusion.3
  133.8 4.5 fusion.2
  138.3 1.6 fusion.42
  139.9 0.5 fusion.27
  140.9 0.4 fusion.71
  141.2 0.6 copy-done
  141.8 1.8 fusion.16
  143.8 0.7 fusion.62
  144.9 1.0 fusion.11
  146.1 0.4 fusion.66
  146.7 0.4 copy-done.4
  147.1 2.3 bitcast_multiply_fusion.5
  149.6 0.4 bitcast_multiply_fusion.4
  150.8 1.2 bitcast_multiply_fusion.3
  153.3 2.4 fusion.34
  156.4 0.4 fusion.44
  156.8 1.0 fusion.35
  157.7 0.5 fusion.31
  158.2 0.5 pad_add_fusion
  158.7 1.6 copy.47
  160.4 3.1 broadcast_in_dim.37
  163.5 96.8 %dynamic_update_slice.10 = f32[2,512,1024]{2,0,1:T(2,128)} dynamic-update-slice(f32[2,512,1024]{2,0,1:T(2,128)} %broadcast_in_dim.37, f32[2,512,512]{2,0,1:T(2,128)S(1)} %copy.47, s32[]{:T(128)} %constant.100.clone.1, s32[]{:T(128)} %constant.100.clone.1, s32[]{:T(128)S(6)} %select_n.79) | dynamic-update-slice | bytes 4194308 | tf_op jit(solution)/shard_map/while/body/eval_jaxpr/transpose(jvp(jit(_roll_dynamic)))/dynamic_update_slice | solution.py:36
  260.3 1.1 broadcast_in_dim.36
  261.4 1.1 copy-done.3
  262.5 1.2 fusion.4
  263.7 1.1 slice_add_fusion.1
  264.8 0.5 fusion.6
  265.3 0.6 fusion.5
  265.9 0.7 broadcast_in_dim.42
  266.6 3.9 pad_maximum_fusion.1
  270.6 0.6 dynamic-slice
  271.8 70.0 %all-reduce.39.cloned.1.call-done = f32[3,512,512]{2,0,1:T(4,128)} async-done(((f32[3,512,512]{2,0,1:T(4,128)}), f32[3,512,512]{2,0,1:T(4,128)}) %all-reduce.39.cloned.1.call-update) | async-done | bytes 3145744
  341.8 1.0 constant_dynamic-slice_fusion.1
  342.9 0.9 collective-permute-start.2
  343.7 1.6 collective-permute-start.3
  345.3 1.1 constant_dynamic-slice_fusion.2
  346.5 1.7 collective-permute-done.3
  348.3 12.3 gather_fusion
  360.6 15.5 %copy.49 = f32[32,3,64,512]{3,2,1,0:T(8,128)} copy(f32[32,3,64,512]{3,1,2,0:T(4,128)} %gather_fusion) | data formatting | bytes 25165824 | tf_op jit(solution)/shard_map/vmap()/gather | solution.py:74
  376.1 1.3 collective-permute-start.4
  377.4 268.0 %collective-permute-done.4 = f32[32,3,64,512]{3,2,1,0:T(8,128)S(1)} collective-permute-done((f32[32,3,64,512]{3,2,1,0:T(8,128)}, f32[32,3,64,512]{3,2,1,0:T(8,128)S(1)}, u32[]{:S(2)}, u32[]{:S(2)}) %collective-permute-start.4) | collective-permute-done | bytes 12582944 | tf_op jit(solution)/shard_map/ppermute | solution.py:79
  645.4 9.7 copy_add_fusion
  655.1 2.8 collective-permute-start.5
  657.9 267.0 %collective-permute-done.5 = f32[32,3,64,512]{3,2,1,0:T(8,128)} collective-permute-done((f32[32,3,64,512]{3,2,1,0:T(8,128)S(1)}, f32[32,3,64,512]{3,2,1,0:T(8,128)}, u32[]{:S(2)}, u32[]{:S(2)}) %collective-permute-start.5) | collective-permute-done | bytes 12582944 | tf_op jit(solution)/shard_map/ppermute | solution.py:79
  924.9 7.1 add.279
  932.0 1.3 collective-permute-start.6
  933.3 266.1 %collective-permute-done.6 = f32[32,3,64,512]{3,2,1,0:T(8,128)} collective-permute-done((f32[32,3,64,512]{3,2,1,0:T(8,128)S(1)}, f32[32,3,64,512]{3,2,1,0:T(8,128)}, u32[]{:S(2)}, u32[]{:S(2)}) %collective-permute-start.6) | collective-permute-done | bytes 12582944 | tf_op jit(solution)/shard_map/ppermute | solution.py:79
  1199.4 6.5 add.280
  1206.0 2.9 collective-permute-start.7
  1208.8 1.7 copy-done.1
  1210.5 263.3 %collective-permute-done.7 = f32[32,3,64,512]{3,2,1,0:T(8,128)S(1)} collective-permute-done((f32[32,3,64,512]{3,2,1,0:T(8,128)S(1)}, f32[32,3,64,512]{3,2,1,0:T(8,128)S(1)}, u32[]{:S(2)}, u32[]{:S(2)}) %collective-permute-start.7) | collective-permute-done | bytes 12582944 | tf_op jit(solution)/shard_map/ppermute | solution.py:79
  1473.8 6.8 add.281
  1480.6 0.8 fusion.1
  1481.4 7.0 fusion
  (45 shorter events, 4.6 us)
Async XLA Ops:
  6.5 121.5 %all-gather.2.cloned.1.call-start = ((), (), s32[]{:S(2)}) async-start(), calls=%async_computation | async-start | bytes 2359296 | tf_op jit(solution)/shard_map/all_gather | solution.py:57
  20.9 5.4 copy-start.6
  23.2 26.0 %collective-permute-start = (f32[32,2,16,512]{3,1,0,2:T(2,128)S(1)}, f32[32,2,16,512]{3,1,0,2:T(2,128)S(1)}, u32[]{:S(2)}, u32[]{:S(2)}) collective-permute-start(f32[32,2,16,512]{3,1,0,2:T(2,128)S(1)} %get-tuple-element.41), channel_id=1, source_target_pairs={{0,1},{1,2},{2,3},{3,4},{4,5},{5,6},{6,7},{7,0},{8,9},{9,10},{10,1... | collective-permute-start | bytes 6291464 | tf_op jit(solution)/shard_map/ppermute | solution.py:19
  26.2 25.5 %collective-permute-start.1 = (f32[32,2,16,512]{3,1,0,2:T(2,128)S(1)}, f32[32,2,16,512]{3,1,0,2:T(2,128)S(1)}, u32[]{:S(2)}, u32[]{:S(2)}) collective-permute-start(f32[32,2,16,512]{3,1,0,2:T(2,128)S(1)} %get-tuple-element.42), channel_id=1, source_target_pairs={{1,0},{2,1},{3,2},{4,3},{5,4},{6,5},{7,6},{0,7},{9,8},{10,9},{11,1... | collective-permute-start | bytes 6291464 | tf_op jit(solution)/shard_map/ppermute | solution.py:20
  93.9 7.1 copy-start.5
  100.7 241.1 %all-reduce.39.cloned.1.call-start = ((), (), s32[]{:S(2)}) async-start(), calls=%async_computation.1 | async-start | bytes 8388608
  133.8 6.1 copy-start.2
  140.6 1.2 copy-start
  146.1 1.0 copy-start.4
  260.3 2.2 copy-start.3
  266.6 3.9 copy-start.7
  342.9 3.6 collective-permute-start.2
  343.7 4.4 collective-permute-start.3
  376.1 269.3 %collective-permute-start.4 = (f32[32,3,64,512]{3,2,1,0:T(8,128)}, f32[32,3,64,512]{3,2,1,0:T(8,128)S(1)}, u32[]{:S(2)}, u32[]{:S(2)}) collective-permute-start(f32[32,3,64,512]{3,2,1,0:T(8,128)} %copy.49), channel_id=1, source_target_pairs={{0,8},{8,0},{16,24},{24,16},{32,40},{40,32},{48,56},{56,48},{64,72... | collective-permute-start | bytes 37748744 | tf_op jit(solution)/shard_map/ppermute | solution.py:79
  655.1 269.8 %collective-permute-start.5 = (f32[32,3,64,512]{3,2,1,0:T(8,128)S(1)}, f32[32,3,64,512]{3,2,1,0:T(8,128)}, u32[]{:S(2)}, u32[]{:S(2)}) collective-permute-start(f32[32,3,64,512]{3,2,1,0:T(8,128)S(1)} %copy_add_fusion), channel_id=1, source_target_pairs={{0,16},{8,24},{16,0},{24,8},{32,48},{40,56},{48,32},{56,40},{64,80... | collective-permute-start | bytes 37748744 | tf_op jit(solution)/shard_map/ppermute | solution.py:79
  932.0 267.4 %collective-permute-start.6 = (f32[32,3,64,512]{3,2,1,0:T(8,128)S(1)}, f32[32,3,64,512]{3,2,1,0:T(8,128)}, u32[]{:S(2)}, u32[]{:S(2)}) collective-permute-start(f32[32,3,64,512]{3,2,1,0:T(8,128)S(1)} %add.279), channel_id=1, source_target_pairs={{0,32},{8,40},{16,48},{24,56},{32,0},{40,8},{48,16},{56,24},{64,96... | collective-permute-start | bytes 37748744 | tf_op jit(solution)/shard_map/ppermute | solution.py:79
  1205.9 4.6 copy-start.1
  1206.0 267.9 %collective-permute-start.7 = (f32[32,3,64,512]{3,2,1,0:T(8,128)S(1)}, f32[32,3,64,512]{3,2,1,0:T(8,128)S(1)}, u32[]{:S(2)}, u32[]{:S(2)}) collective-permute-start(f32[32,3,64,512]{3,2,1,0:T(8,128)S(1)} %add.280), channel_id=1, source_target_pairs={{0,64},{8,72},{16,80},{24,88},{32,96},{40,104},{48,112},{56,120},{... | collective-permute-start | bytes 37748744 | tf_op jit(solution)/shard_map/ppermute | solution.py:79
Sparse Core Ops, SparseCore 0:
  100.8 27.1 all-gather.1
  270.7 71.1 all-reduce.38
